TPU v7x, 512 devices: a whole 4x8x8 slice. The times are simulated.
512 devices in a mesh: gs: 128 (over y, z, core), view: 4 (over x).
Axes of the slice: x: 4, y: 8, z: 8, core: 2. Of those that a mesh axis runs over, the one named last changes fastest.
Arguments:
- features: bfloat16 [131072, 128], P('gs'), may hold values from -6 to 6
- geometry: float32 [4, 9, 131072], P('view', None, 'gs'), as said below
- decoder: bfloat16 [128, 512], replicated, may hold values from -0.5 to 0.5
- teacher: bfloat16 [4, 131072, 512], P('view', 'gs'), may hold values from -3 to 3
- images: float32 [4, 3, 131072], P('view', None, 'gs'), may hold values from 0 to 1
- send_index: int32 [4, 128, 1024], P('view', 'gs'), may hold values from 0 to 1023, as said below
- tile_lists: int32 [4, 512, 8], P('view', 'gs'), may hold values from 0 to 7, as said below
- tile_lengths: int32 [4, 512], P('view', 'gs'), may hold values from 2 to 8
Outputs:
- feature_grad: float32 [131072, 128], P(('gs', 'view'))
- geometry_grad: float32 [4, 9, 131072], P('view', None, 'gs')
- decoder_grad: float32 [128, 512], replicated
Inputs may be any that keep to these rules, and one draw needn't show every extreme that they name: `send_index`: each row (one view, one source device) is a permutation of 0 .. 1023; positions k * 8 to (k + 1) * 8 - 1 hold the Gaussians sent to the device of gs index k. `tile_lists`: the 8 entries of a row are distinct. `geometry`: opacity logits lie in -7.5 .. -4, log conics between -2 log 16 and -2 log 16 + 2 log 4, shears in -2 .. 2, colors in 0 .. 1.
All inputs are finite; a program needn't handle non-finite values.
Results may differ from a plain program's by a relative error of at most 0.0017.
Values may be sent and summed in bfloat16 or wider, within the bound.
A program may use at most 64 MiB of HBM per device.

v0:
```python
import math
import jax
import jax.numpy as jnp
from jax import lax
from jax.sharding import PartitionSpec as P

FEAT = 128
CT = 512
TS = 16
BLK = 128
LIST = 8


def composite(tile_geo, alive_mask, pixel_x, pixel_y):
    delta_x = pixel_x[:, None] - tile_geo[0][None, :]
    delta_y = pixel_y[:, None] - tile_geo[1][None, :]
    conic_a = jnp.exp(tile_geo[2])
    conic_c = jnp.exp(tile_geo[3])
    conic_b = 0.8 * jnp.tanh(tile_geo[4]) * jnp.exp(0.5 * (tile_geo[2] + tile_geo[3]))
    exponent = -0.5 * (
        conic_a * delta_x * delta_x
        + 2.0 * conic_b * delta_x * delta_y
        + conic_c * delta_y * delta_y
    )
    opacity = alive_mask * jax.nn.sigmoid(tile_geo[5])
    alpha_val = opacity[None, :] * jnp.exp(exponent)
    log_keep = jnp.log1p(-alpha_val)
    pixel_count = pixel_x.shape[0]
    blocked = log_keep.reshape(pixel_count, LIST, BLK)
    inner = jnp.cumsum(blocked, axis=2) - blocked
    block_sums = jnp.sum(blocked, axis=2)
    outer = jnp.cumsum(block_sums, axis=1) - block_sums
    before = (inner + outer[:, :, None]).reshape(pixel_count, LIST * BLK)
    weights = alpha_val * jnp.exp(before)
    pixel_color = jnp.einsum("pi,ci->cp", weights, tile_geo[6:9], precision=lax.Precision.HIGHEST)
    return (weights, pixel_color)


def device_terms(
    recv_geo, recv_feat, decoder, teacher_dev, images_dev, lists, lengths, shard_index
):
    nblocks = recv_feat.shape[0] // BLK
    tile_pixels = TS * TS
    geo_blocks = recv_geo.reshape(9, nblocks, BLK)
    feat_blocks = recv_feat.reshape(nblocks, BLK, FEAT)
    within = jnp.arange(tile_pixels, dtype=jnp.int32)
    block_range = jnp.arange(nblocks, dtype=jnp.int32)
    slot_range = jnp.arange(LIST, dtype=jnp.int32)

    def tile_step(totals, tile_index):
        decoder_sum, geo_acc, feat_acc = totals
        block_ids = lists[tile_index]
        count = lengths[tile_index]
        alive_mask = jnp.broadcast_to(
            (slot_range < count).astype(jnp.float32)[:, None], (LIST, BLK)
        ).reshape(LIST * BLK)
        tile_geo = jnp.take(geo_blocks, block_ids, axis=1).reshape(9, LIST * BLK)
        feat_tile = jnp.take(feat_blocks, block_ids, axis=0).reshape(LIST * BLK, FEAT)
        column = 2 * TS * (shard_index % 30) + TS * (tile_index % 2) + within % TS
        row_index = 2 * TS * (shard_index // 30) + TS * (tile_index // 2) + within // TS
        pixel_x = column.astype(jnp.float32) + 0.5
        pixel_y = row_index.astype(jnp.float32) + 0.5
        (weights, pixel_color), pullback = jax.vjp(
            lambda geo_part: composite(geo_part, alive_mask, pixel_x, pixel_y), tile_geo
        )
        weight_b = weights.astype(jnp.bfloat16)
        rendered = jnp.dot(weight_b, feat_tile, preferred_element_type=jnp.float32).astype(
            jnp.bfloat16
        )
        pred = jnp.dot(rendered, decoder, preferred_element_type=jnp.float32)
        teacher_rows = lax.dynamic_slice_in_dim(
            teacher_dev, tile_index * tile_pixels, tile_pixels, 0
        )
        error_feat = pred - teacher_rows.astype(jnp.float32)
        gpred = (error_feat / jnp.sqrt(error_feat * error_feat + 0.04)).astype(jnp.bfloat16)
        grender = lax.dot_general(
            gpred, decoder, (((1,), (1,)), ((), ())), preferred_element_type=jnp.float32
        ).astype(jnp.bfloat16)
        decoder_sum = decoder_sum + lax.dot_general(
            rendered, gpred, (((0,), (0,)), ((), ())), preferred_element_type=jnp.float32
        )
        image_cols = lax.dynamic_slice_in_dim(images_dev, tile_index * tile_pixels, tile_pixels, 1)
        error_color = pixel_color - image_cols
        gcolor = error_color / jnp.sqrt(error_color * error_color + 0.04)
        gweight = lax.dot_general(
            grender, feat_tile, (((1,), (1,)), ((), ())), preferred_element_type=jnp.float32
        )
        gfeat_tile = lax.dot_general(
            weight_b, grender, (((0,), (0,)), ((), ())), preferred_element_type=jnp.float32
        )
        (ggeo_tile,) = pullback((gweight, gcolor))
        hits = (block_ids[:, None] == block_range[None, :]).astype(jnp.float32)
        geo_acc = geo_acc + jnp.einsum(
            "clb,ln->cnb", ggeo_tile.reshape(9, LIST, BLK), hits, precision=lax.Precision.HIGHEST
        )
        feat_acc = feat_acc + jnp.einsum(
            "ln,lbf->nbf",
            hits,
            gfeat_tile.reshape(LIST, BLK, FEAT),
            precision=lax.Precision.HIGHEST,
        )
        return ((decoder_sum, geo_acc, feat_acc), None)

    start_totals = (
        jnp.zeros((FEAT, CT), jnp.float32),
        jnp.zeros((9, nblocks, BLK), jnp.float32),
        jnp.zeros((nblocks, BLK, FEAT), jnp.float32),
    )
    tile_range = jnp.arange(lists.shape[0], dtype=jnp.int32)
    (decoder_sum, geo_acc, feat_acc), _ = lax.scan(tile_step, start_totals, tile_range)
    return (decoder_sum, geo_acc.reshape(9, nblocks * BLK), feat_acc.reshape(nblocks * BLK, FEAT))


def on_device(features, geometry, decoder, teacher, images, send_index, tile_lists, tile_lengths):
    send_order = send_index[0, 0]
    shard_index = lax.axis_index("gs")
    geo_send = jnp.take(geometry[0], send_order, axis=1)
    recv_geo = lax.all_to_all(geo_send, "gs", split_axis=1, concat_axis=1, tiled=True)
    feat_send = jnp.take(features, send_order, axis=0)
    recv_feat = lax.all_to_all(feat_send, "gs", split_axis=0, concat_axis=0, tiled=True)
    decoder_sum, geo_acc, feat_acc = device_terms(
        recv_geo,
        recv_feat,
        decoder,
        teacher[0],
        images[0],
        tile_lists[0],
        tile_lengths[0],
        shard_index,
    )
    returned_geo = lax.all_to_all(geo_acc, "gs", split_axis=1, concat_axis=1, tiled=True)
    returned_feat = lax.all_to_all(feat_acc, "gs", split_axis=0, concat_axis=0, tiled=True)
    geo_own = jnp.zeros_like(returned_geo).at[:, send_order].set(returned_geo)
    feat_own = jnp.zeros_like(returned_feat).at[send_order].set(returned_feat)
    quarter = feat_own.shape[0] // lax.axis_size("view")
    summed = lax.psum(feat_own, "view")
    feature_grad = lax.dynamic_slice_in_dim(summed, lax.axis_index("view") * quarter, quarter, 0)
    pixel_total = lax.axis_size("gs") * lax.axis_size("view") * tile_lists.shape[1] * TS * TS
    decoder_grad = lax.psum(decoder_sum, ("gs", "view")) * (1.0 / math.sqrt(pixel_total))
    return (feature_grad, geo_own[None], decoder_grad)


def solution(mesh):
    placed = (
        P("gs", None),
        P("view", None, "gs"),
        P(),
        P("view", "gs", None),
        P("view", None, "gs"),
        P("view", "gs", None),
        P("view", "gs", None),
        P("view", "gs"),
    )
    return jax.shard_map(
        on_device,
        mesh=mesh,
        in_specs=placed,
        out_specs=(P(("gs", "view"), None), P("view", None, "gs"), P()),
        check_vma=False,
    )
```

profile of v0, /device:TPU:8, one launch (start us, length us, event | category | flops | bytes accessed | tf_op | source)
XLA Modules:
  0.0 610.4 jit_solution(10011325874883574381)
XLA Ops:
  10.2 2.8 gather_fusion.2
  14.1 17.4 %all-to-all-start = ((f32[9,128,8]{0,2,1:T(8,128)}), f32[9,128,8]{0,2,1:T(8,128)S(1)}, u32[]{:S(2)}, u32[]{:S(2)}) async-start(f32[9,128,8]{0,2,1:T(8,128)} %bitcast_select_fusion.1), calls=%async_computation | async-start | bytes 1048576 | tf_op jit(solution)/shard_map/all_to_all | solution.py:118
  31.5 3.2 gather_fusion.3
  35.6 16.2 %all-to-all-done = f32[9,128,8]{0,2,1:T(8,128)S(1)} async-done(((f32[9,128,8]{0,2,1:T(8,128)}), f32[9,128,8]{0,2,1:T(8,128)S(1)}, u32[]{:S(2)}, u32[]{:S(2)}) %all-to-all-start) | async-done | bytes 36896 | tf_op jit(solution)/shard_map/all_to_all | solution.py:118
  51.8 6.5 %all-to-all-start.1 = ((bf16[128,8,128]{2,1,0:T(8,128)(2,1)}), bf16[128,8,128]{2,1,0:T(8,128)(2,1)S(1)}, u32[]{:S(2)}, u32[]{:S(2)}) async-start(bf16[128,8,128]{2,1,0:T(8,128)(2,1)} %bitcast_select_fusion.2), calls=%async_computation.1 | async-start | bytes 524288 | tf_op jit(solution)/shard_map/all_to_all | solution.py:120
  60.4 12.6 %all-to-all-done.1 = bf16[128,8,128]{2,1,0:T(8,128)(2,1)S(1)} async-done(((bf16[128,8,128]{2,1,0:T(8,128)(2,1)}), bf16[128,8,128]{2,1,0:T(8,128)(2,1)S(1)}, u32[]{:S(2)}, u32[]{:S(2)}) %all-to-all-start.1) | async-done | bytes 262176 | tf_op jit(solution)/shard_map/all_to_all | solution.py:120
  73.7 187.1 %while.21 = (s32[]{:T(128)}, f32[128,512]{1,0:T(8,128)}, f32[9,8,128]{2,1,0:T(8,128)}, f32[8,128,128]{2,0,1:T(8,128)}, s32[4]{0:T(128)S(1)}, /*index=5*/s32[4]{0...) while((s32[]{:T(128)}, f32[128,512]{1,0:T(8,128)}, ...), condition=%wide.region_13.14_spmd.clone.clone, body=%wide.region_0.13_spmd.clone.clone.sunk | while | flops 448201472 | bytes 62394652 | solution.py:110
  107.0 3.4 fusion.167
  114.7 2.3 fusion.168
  154.0 3.4 fusion.167
  161.7 2.3 fusion.168
  194.7 2.3 convolution_add_fusion.8
  201.1 3.4 fusion.167
  208.8 2.3 fusion.168
  248.1 3.4 fusion.167
  255.8 2.3 fusion.168
  262.7 6.5 %all-to-all-start.2 = ((f32[128,8,128]{2,1,0:T(8,128)}), f32[128,8,128]{2,1,0:T(8,128)S(1)}, u32[]{:S(2)}, u32[]{:S(2)}) async-start(f32[128,8,128]{2,1,0:T(8,128)} %bitcast.11), calls=%async_computation.2 | async-start | bytes 1048576 | tf_op jit(solution)/shard_map/all_to_all | solution.py:132
  270.0 19.5 %all-to-all-done.2 = f32[128,8,128]{2,1,0:T(8,128)S(1)} async-done(((f32[128,8,128]{2,1,0:T(8,128)}), f32[128,8,128]{2,1,0:T(8,128)S(1)}, u32[]{:S(2)}, u32[]{:S(2)}) %all-to-all-start.2) | async-done | bytes 524320 | tf_op jit(solution)/shard_map/all_to_all | solution.py:132
  289.5 4.0 scatter_custom_fusion
  295.4 6.4 %all-to-all-start.3 = ((f32[9,128,8]{0,2,1:T(8,128)}), f32[9,128,8]{0,2,1:T(8,128)S(1)}, u32[]{:S(2)}, u32[]{:S(2)}) async-start(f32[9,128,8]{0,2,1:T(8,128)} %bitcast.13), calls=%async_computation.3 | async-start | bytes 1048576 | tf_op jit(solution)/shard_map/all_to_all | solution.py:131
  301.7 20.4 %all-to-all-done.3 = f32[9,128,8]{0,2,1:T(8,128)S(1)} async-done(((f32[9,128,8]{0,2,1:T(8,128)}), f32[9,128,8]{0,2,1:T(8,128)S(1)}, u32[]{:S(2)}, u32[]{:S(2)}) %all-to-all-start.3) | async-done | bytes 36896 | tf_op jit(solution)/shard_map/all_to_all | solution.py:131
  322.2 3.4 scatter_custom_fusion.1
  326.4 222.5 %all-reduce.14.cloned.1.call-done = f32[128,512]{1,0:T(8,128)} async-done(((f32[128,512]{1,0:T(8,128)}), f32[128,512]{1,0:T(8,128)}) %all-reduce.14.cloned.1.call-update) | async-done | bytes 262160 | tf_op jit(solution)/shard_map/psum | solution.py:139
  550.5 51.4 %all-reduce.12.cloned.1.call-done = f32[1024,128]{1,0:T(8,128)} async-done(((f32[1024,128]{1,0:T(8,128)}), f32[1024,128]{1,0:T(8,128)}) %all-reduce.12.cloned.1.call-update) | async-done | bytes 524304 | tf_op jit(solution)/shard_map/psum | solution.py:136
  (525 shorter events, 158.1 us)
Async XLA Ops:
  7.2 24.3 %copy-start = (bf16[1024,128]{1,0:T(8,128)(2,1)S(1)}, bf16[1024,128]{1,0:T(8,128)(2,1)}, u32[]{:S(2)}) copy-start(bf16[1024,128]{1,0:T(8,128)(2,1)} %param.10) | copy-start | bytes 786436
  14.1 37.7 %all-to-all-start = ((f32[9,128,8]{0,2,1:T(8,128)}), f32[9,128,8]{0,2,1:T(8,128)S(1)}, u32[]{:S(2)}, u32[]{:S(2)}) async-start(f32[9,128,8]{0,2,1:T(8,128)} %bitcast_select_fusion.1), calls=%async_computation | async-start | bytes 1048576 | tf_op jit(solution)/shard_map/all_to_all | solution.py:118
  51.8 21.3 %all-to-all-start.1 = ((bf16[128,8,128]{2,1,0:T(8,128)(2,1)}), bf16[128,8,128]{2,1,0:T(8,128)(2,1)S(1)}, u32[]{:S(2)}, u32[]{:S(2)}) async-start(bf16[128,8,128]{2,1,0:T(8,128)(2,1)} %bitcast_select_fusion.2), calls=%async_computation.1 | async-start | bytes 524288 | tf_op jit(solution)/shard_map/all_to_all | solution.py:120
  81.3 22.9 %copy-start.21 = (f32[256]{0:T(256)}, f32[256]{0:T(256)S(1)}, u32[]{:S(2)}) copy-start(f32[256]{0:T(256)S(1)} %get-tuple-element.768) | copy-start | bytes 3076 | tf_op jit(solution)/shard_map/while
  81.3 22.9 %copy-start.23 = (f32[256]{0:T(256)}, f32[256]{0:T(256)S(1)}, u32[]{:S(2)}) copy-start(f32[256]{0:T(256)S(1)} %get-tuple-element.765) | copy-start | bytes 3076 | tf_op jit(solution)/shard_map/while
  127.3 24.0 %copy-start.21 = (f32[256]{0:T(256)}, f32[256]{0:T(256)S(1)}, u32[]{:S(2)}) copy-start(f32[256]{0:T(256)S(1)} %get-tuple-element.768) | copy-start | bytes 3076 | tf_op jit(solution)/shard_map/while
  127.3 24.0 %copy-start.23 = (f32[256]{0:T(256)}, f32[256]{0:T(256)S(1)}, u32[]{:S(2)}) copy-start(f32[256]{0:T(256)S(1)} %get-tuple-element.765) | copy-start | bytes 3076 | tf_op jit(solution)/shard_map/while
  130.2 20.0 %copy-start.5 = (f32[9,8,128]{2,0,1:T(8,128)}, f32[9,8,128]{2,0,1:T(8,128)S(1)}, u32[]{:S(2)}) copy-start(f32[9,8,128]{2,0,1:T(8,128)S(1)} %select_bitcast_fusion.2) | copy-start | bytes 110596 | tf_op jit(solution)/shard_map/while
  130.8 20.5 %copy-start.11 = (f32[1,8,128]{2,0,1:T(1,128)}, f32[1,8,128]{2,0,1:T(1,128)S(1)}, u32[]{:S(2)}) copy-start(f32[1,8,128]{2,0,1:T(1,128)S(1)} %get-tuple-element.769) | copy-start | bytes 12292 | tf_op jit(solution)/shard_map/while
  131.4 19.9 %copy-start.16 = (f32[1024]{0:T(1024)}, f32[1024]{0:T(1024)S(1)}, u32[]{:S(2)}) copy-start(f32[1024]{0:T(1024)S(1)} %bitcast_multiply_fusion.8) | copy-start | bytes 12292 | tf_op jit(solution)/shard_map/while
  174.3 24.0 %copy-start.21 = (f32[256]{0:T(256)}, f32[256]{0:T(256)S(1)}, u32[]{:S(2)}) copy-start(f32[256]{0:T(256)S(1)} %get-tuple-element.768) | copy-start | bytes 3076 | tf_op jit(solution)/shard_map/while
  174.3 24.0 %copy-start.23 = (f32[256]{0:T(256)}, f32[256]{0:T(256)S(1)}, u32[]{:S(2)}) copy-start(f32[256]{0:T(256)S(1)} %get-tuple-element.765) | copy-start | bytes 3076 | tf_op jit(solution)/shard_map/while
  177.2 20.0 %copy-start.5 = (f32[9,8,128]{2,0,1:T(8,128)}, f32[9,8,128]{2,0,1:T(8,128)S(1)}, u32[]{:S(2)}) copy-start(f32[9,8,128]{2,0,1:T(8,128)S(1)} %select_bitcast_fusion.2) | copy-start | bytes 110596 | tf_op jit(solution)/shard_map/while
  177.8 20.5 %copy-start.11 = (f32[1,8,128]{2,0,1:T(1,128)}, f32[1,8,128]{2,0,1:T(1,128)S(1)}, u32[]{:S(2)}) copy-start(f32[1,8,128]{2,0,1:T(1,128)S(1)} %get-tuple-element.769) | copy-start | bytes 12292 | tf_op jit(solution)/shard_map/while
  178.4 19.9 %copy-start.16 = (f32[1024]{0:T(1024)}, f32[1024]{0:T(1024)S(1)}, u32[]{:S(2)}) copy-start(f32[1024]{0:T(1024)S(1)} %bitcast_multiply_fusion.8) | copy-start | bytes 12292 | tf_op jit(solution)/shard_map/while
  221.3 24.0 %copy-start.21 = (f32[256]{0:T(256)}, f32[256]{0:T(256)S(1)}, u32[]{:S(2)}) copy-start(f32[256]{0:T(256)S(1)} %get-tuple-element.768) | copy-start | bytes 3076 | tf_op jit(solution)/shard_map/while
  221.3 24.0 %copy-start.23 = (f32[256]{0:T(256)}, f32[256]{0:T(256)S(1)}, u32[]{:S(2)}) copy-start(f32[256]{0:T(256)S(1)} %get-tuple-element.765) | copy-start | bytes 3076 | tf_op jit(solution)/shard_map/while
  224.2 20.0 %copy-start.5 = (f32[9,8,128]{2,0,1:T(8,128)}, f32[9,8,128]{2,0,1:T(8,128)S(1)}, u32[]{:S(2)}) copy-start(f32[9,8,128]{2,0,1:T(8,128)S(1)} %select_bitcast_fusion.2) | copy-start | bytes 110596 | tf_op jit(solution)/shard_map/while
  224.9 20.5 %copy-start.11 = (f32[1,8,128]{2,0,1:T(1,128)}, f32[1,8,128]{2,0,1:T(1,128)S(1)}, u32[]{:S(2)}) copy-start(f32[1,8,128]{2,0,1:T(1,128)S(1)} %get-tuple-element.769) | copy-start | bytes 12292 | tf_op jit(solution)/shard_map/while
  225.5 19.9 %copy-start.16 = (f32[1024]{0:T(1024)}, f32[1024]{0:T(1024)S(1)}, u32[]{:S(2)}) copy-start(f32[1024]{0:T(1024)S(1)} %bitcast_multiply_fusion.8) | copy-start | bytes 12292 | tf_op jit(solution)/shard_map/while
  262.7 26.8 %all-to-all-start.2 = ((f32[128,8,128]{2,1,0:T(8,128)}), f32[128,8,128]{2,1,0:T(8,128)S(1)}, u32[]{:S(2)}, u32[]{:S(2)}) async-start(f32[128,8,128]{2,1,0:T(8,128)} %bitcast.11), calls=%async_computation.2 | async-start | bytes 1048576 | tf_op jit(solution)/shard_map/all_to_all | solution.py:132
  269.2 279.6 %all-reduce.14.cloned.1.call-start = ((), (), s32[]{:S(2)}) async-start(), calls=%async_computation.5 | async-start | bytes 524288 | tf_op jit(solution)/shard_map/psum | solution.py:139
  269.9 332.0 %all-reduce.12.cloned.1.call-start = ((), (), s32[]{:S(2)}) async-start(), calls=%async_computation.4 | async-start | bytes 1048576 | tf_op jit(solution)/shard_map/psum | solution.py:136
  295.4 26.8 %all-to-all-start.3 = ((f32[9,128,8]{0,2,1:T(8,128)}), f32[9,128,8]{0,2,1:T(8,128)S(1)}, u32[]{:S(2)}, u32[]{:S(2)}) async-start(f32[9,128,8]{0,2,1:T(8,128)} %bitcast.13), calls=%async_computation.3 | async-start | bytes 1048576 | tf_op jit(solution)/shard_map/all_to_all | solution.py:131
  (113 other events, 331.2 us)
Sparse Core Ops, SparseCore 0:
  275.6 273.1 all-reduce.13
  551.3 50.6 all-reduce.11
where the time goes:
time: 613 us; the launch traced here: 610 us
  waiting for transfers between devices  343 us (56%)
  local copies, waits for them, and re-layouts  79.9 us (13%)
  other arithmetic  76.6 us (12%)
  matrix products  39.1 us (6%)
  starting transfers between devices  36.8 us (6%)
  loops' own time  20.3 us (3%)
  between operations  14.3 us (2%)
    psum x1, waiting for transfers between devices, on_device(): lax.psum(decoder_sum, ('gs', 'view')) * (1.0 / math.sqrt(pixel_total))  222 us
    psum x1, waiting for transfers between devices, on_device(): summed = lax.psum(feat_own, 'view')  51.4 us
    another operation x8, other arithmetic, composite(): inner = jnp.cumsum(blocked, axis=2) - blocked  22.4 us
    all_to_all x1, waiting for transfers between devices, on_device(): lax.all_to_all(geo_acc, 'gs', split_axis=1, concat_axis=1, tiled=True)  20.4 us
    another operation x1, loops' own time, device_terms(): lax.scan(tile_step, start_totals, tile_range)  20.3 us
    all_to_all x1, waiting for transfers between devices, on_device(): lax.all_to_all(feat_acc, 'gs', split_axis=0, concat_axis=0, tiled=True)  19.5 us
    while x264, local copies, waits for them, and re-layouts  19.3 us
    all_to_all x1, starting transfers between devices, on_device(): lax.all_to_all(geo_send, 'gs', split_axis=1, concat_axis=1, tiled=True)  17.4 us
  transfers between devices with their start and end apart: 6, of which 6 were waited for; matrix products, arithmetic and copies ran while one was open for 3% of the time, Pallas kernels for 0%

commit v1 on v0

--- a/solution.py
+++ b/solution.py
@@ -133,7 +133,7 @@
     geo_own = jnp.zeros_like(returned_geo).at[:, send_order].set(returned_geo)
     feat_own = jnp.zeros_like(returned_feat).at[send_order].set(returned_feat)
     quarter = feat_own.shape[0] // lax.axis_size("view")
-    summed = lax.psum(feat_own, "view")
+    summed = jnp.sum(lax.all_gather(feat_own, "view"), axis=0)
     feature_grad = lax.dynamic_slice_in_dim(summed, lax.axis_index("view") * quarter, quarter, 0)
     pixel_total = lax.axis_size("gs") * lax.axis_size("view") * tile_lists.shape[1] * TS * TS
     decoder_grad = lax.psum(decoder_sum, ("gs", "view")) * (1.0 / math.sqrt(pixel_total))

time: 613 us -> 572 us (0.933)
  the two profiles are of different devices: /device:TPU:8 before, /device:TPU:23 now
where the time goes in v1:
time: 572 us; the launch traced here: 569 us
  waiting for transfers between devices  288 us (50%)
  other arithmetic  81.8 us (14%)
  local copies, waits for them, and re-layouts  74 us (13%)
  starting transfers between devices  44.8 us (8%)
  matrix products  44.6 us (8%)
  loops' own time  20.1 us (4%)
  between operations  15.7 us (3%)
    psum x1, waiting for transfers between devices, on_device(): lax.psum(decoder_sum, ('gs', 'view')) * (1.0 / math.sqrt(pixel_total))  227 us
    another operation x8, other arithmetic, composite(): inner = jnp.cumsum(blocked, axis=2) - blocked  22.4 us
    another operation x1, loops' own time, device_terms(): lax.scan(tile_step, start_totals, tile_range)  20.1 us
    all_to_all x1, waiting for transfers between devices, on_device(): lax.all_to_all(geo_acc, 'gs', split_axis=1, concat_axis=1, tiled=True)  18 us
    all_to_all x1, starting transfers between devices, on_device(): lax.all_to_all(geo_send, 'gs', split_axis=1, concat_axis=1, tiled=True)  17.8 us
    dot_general x12, matrix products, composite(): jnp.einsum('pi,ci->cp', weights, tile_geo[6:9], precision=lax.Precision.H...  17.3 us
    all_to_all x1, waiting for transfers between devices, on_device(): lax.all_to_all(feat_acc, 'gs', split_axis=0, concat_axis=0, tiled=True)  17.1 us
    all_to_all x1, waiting for transfers between devices, on_device(): lax.all_to_all(geo_send, 'gs', split_axis=1, concat_axis=1, tiled=True)  13.8 us
  transfers between devices with their start and end apart: 6, of which 5 were waited for; matrix products, arithmetic and copies ran while one was open for 3% of the time, Pallas kernels for 0%

profile of v1, /device:TPU:23, one launch (start us, length us, event | category | flops | bytes accessed | tf_op | source)
XLA Modules:
  0.0 569.2 jit_solution(16678067210179080570)
XLA Ops:
  11.7 2.8 gather_fusion.2
  15.6 17.8 %all-to-all-start = ((f32[9,128,8]{0,2,1:T(8,128)}), f32[9,128,8]{0,2,1:T(8,128)S(1)}, u32[]{:S(2)}, u32[]{:S(2)}) async-start(f32[9,128,8]{0,2,1:T(8,128)} %bitcast_select_fusion.1), calls=%async_computation | async-start | bytes 1048576 | tf_op jit(solution)/shard_map/all_to_all | solution.py:118
  33.4 3.2 gather_fusion.3
  37.5 13.8 %all-to-all-done = f32[9,128,8]{0,2,1:T(8,128)S(1)} async-done(((f32[9,128,8]{0,2,1:T(8,128)}), f32[9,128,8]{0,2,1:T(8,128)S(1)}, u32[]{:S(2)}, u32[]{:S(2)}) %all-to-all-start) | async-done | bytes 36896 | tf_op jit(solution)/shard_map/all_to_all | solution.py:118
  51.3 9.9 %all-to-all-start.1 = ((bf16[128,8,128]{2,1,0:T(8,128)(2,1)}), bf16[128,8,128]{2,1,0:T(8,128)(2,1)}, u32[]{:S(2)}, u32[]{:S(2)}) async-start(bf16[128,8,128]{2,1,0:T(8,128)(2,1)} %bitcast_select_fusion.2), calls=%async_computation.1 | async-start | bytes 524288 | tf_op jit(solution)/shard_map/all_to_all | solution.py:120
  62.7 11.3 %all-to-all-done.1 = bf16[128,8,128]{2,1,0:T(8,128)(2,1)} async-done(((bf16[128,8,128]{2,1,0:T(8,128)(2,1)}), bf16[128,8,128]{2,1,0:T(8,128)(2,1)}, u32[]{:S(2)}, u32[]{:S(2)}) %all-to-all-start.1) | async-done | bytes 262176 | tf_op jit(solution)/shard_map/all_to_all | solution.py:120
  74.5 191.7 %while.21 = (s32[]{:T(128)}, f32[128,512]{1,0:T(8,128)}, f32[9,8,128]{2,1,0:T(8,128)}, f32[8,128,128]{2,0,1:T(8,128)}, s32[4]{0:T(128)}, /*index=5*/s32[4]{0:T(1...) while((s32[]{:T(128)}, f32[128,512]{1,0:T(8,128)}, ...), condition=%wide.region_13.14_spmd.clone.clone, body=%wide.region_0.13_spmd.clone.clone.sunk | while | flops 448201472 | bytes 58158880 | solution.py:110
  91.3 2.2 exponential_multiply_fusion.2
  109.0 3.4 fusion.167
  116.1 3.0 fusion.168
  137.8 2.2 exponential_multiply_fusion.2
  157.4 3.4 fusion.167
  164.5 3.0 fusion.168
  205.9 3.4 fusion.167
  212.9 3.0 fusion.168
  254.3 3.4 fusion.167
  261.3 3.0 fusion.168
  268.2 8.1 %all-to-all-start.2 = ((f32[128,8,128]{2,1,0:T(8,128)}), f32[128,8,128]{2,1,0:T(8,128)S(1)}, u32[]{:S(2)}, u32[]{:S(2)}) async-start(f32[128,8,128]{2,1,0:T(8,128)} %bitcast.11), calls=%async_computation.2 | async-start | bytes 1048576 | tf_op jit(solution)/shard_map/all_to_all | solution.py:132
  277.1 17.1 %all-to-all-done.2 = f32[128,8,128]{2,1,0:T(8,128)S(1)} async-done(((f32[128,8,128]{2,1,0:T(8,128)}), f32[128,8,128]{2,1,0:T(8,128)S(1)}, u32[]{:S(2)}, u32[]{:S(2)}) %all-to-all-start.2) | async-done | bytes 524320 | tf_op jit(solution)/shard_map/all_to_all | solution.py:132
  294.2 4.0 scatter_custom_fusion
  299.3 8.8 %all-to-all-start.3 = ((f32[9,128,8]{0,2,1:T(8,128)}), f32[9,128,8]{0,2,1:T(8,128)S(1)}, u32[]{:S(2)}, u32[]{:S(2)}) async-start(f32[9,128,8]{0,2,1:T(8,128)} %bitcast.14), calls=%async_computation.3 | async-start | bytes 1048576 | tf_op jit(solution)/shard_map/all_to_all | solution.py:131
  308.1 18.0 %all-to-all-done.3 = f32[9,128,8]{0,2,1:T(8,128)S(1)} async-done(((f32[9,128,8]{0,2,1:T(8,128)}), f32[9,128,8]{0,2,1:T(8,128)S(1)}, u32[]{:S(2)}, u32[]{:S(2)}) %all-to-all-start.3) | async-done | bytes 36896 | tf_op jit(solution)/shard_map/all_to_all | solution.py:131
  326.1 3.4 scatter_custom_fusion.1
  330.3 227.4 %all-reduce.11.cloned.1.call-done = f32[128,512]{1,0:T(8,128)} async-done(((f32[128,512]{1,0:T(8,128)}), f32[128,512]{1,0:T(8,128)}) %all-reduce.11.cloned.1.call-update) | async-done | bytes 262160 | tf_op jit(solution)/shard_map/psum | solution.py:139
  (432 shorter events, 157.9 us)
Async XLA Ops:
  8.0 25.4 %copy-start = (bf16[1024,128]{1,0:T(8,128)(2,1)S(1)}, bf16[1024,128]{1,0:T(8,128)(2,1)}, u32[]{:S(2)}) copy-start(bf16[1024,128]{1,0:T(8,128)(2,1)} %param.10) | copy-start | bytes 786436
  15.6 45.7 %copy-start.23 = (f32[1,3,1024]{2,0,1:T(1,128)S(1)}, f32[1,3,1024]{2,0,1:T(1,128)}, u32[]{:S(2)}) copy-start(f32[1,3,1024]{2,0,1:T(1,128)} %param.14) | copy-start | bytes 36868
  15.6 35.7 %all-to-all-start = ((f32[9,128,8]{0,2,1:T(8,128)}), f32[9,128,8]{0,2,1:T(8,128)S(1)}, u32[]{:S(2)}, u32[]{:S(2)}) async-start(f32[9,128,8]{0,2,1:T(8,128)} %bitcast_select_fusion.1), calls=%async_computation | async-start | bytes 1048576 | tf_op jit(solution)/shard_map/all_to_all | solution.py:118
  51.3 22.7 %all-to-all-start.1 = ((bf16[128,8,128]{2,1,0:T(8,128)(2,1)}), bf16[128,8,128]{2,1,0:T(8,128)(2,1)}, u32[]{:S(2)}, u32[]{:S(2)}) async-start(bf16[128,8,128]{2,1,0:T(8,128)(2,1)} %bitcast_select_fusion.2), calls=%async_computation.1 | async-start | bytes 524288 | tf_op jit(solution)/shard_map/all_to_all | solution.py:120
  82.9 23.4 %copy-start.15 = (f32[256]{0:T(256)}, f32[256]{0:T(256)S(1)}, u32[]{:S(2)}) copy-start(f32[256]{0:T(256)S(1)} %get-tuple-element.785) | copy-start | bytes 3076 | tf_op jit(solution)/shard_map/while
  82.9 23.4 %copy-start.16 = (f32[256]{0:T(256)}, f32[256]{0:T(256)S(1)}, u32[]{:S(2)}) copy-start(f32[256]{0:T(256)S(1)} %get-tuple-element.782) | copy-start | bytes 3076 | tf_op jit(solution)/shard_map/while
  129.3 25.3 %copy-start.15 = (f32[256]{0:T(256)}, f32[256]{0:T(256)S(1)}, u32[]{:S(2)}) copy-start(f32[256]{0:T(256)S(1)} %get-tuple-element.785) | copy-start | bytes 3076 | tf_op jit(solution)/shard_map/while
  129.3 25.3 %copy-start.16 = (f32[256]{0:T(256)}, f32[256]{0:T(256)S(1)}, u32[]{:S(2)}) copy-start(f32[256]{0:T(256)S(1)} %get-tuple-element.782) | copy-start | bytes 3076 | tf_op jit(solution)/shard_map/while
  132.9 21.8 %copy-start.7 = (f32[1,8,128]{2,0,1:T(1,128)}, f32[1,8,128]{2,0,1:T(1,128)S(1)}, u32[]{:S(2)}) copy-start(f32[1,8,128]{2,0,1:T(1,128)S(1)} %get-tuple-element.786) | copy-start | bytes 12292 | tf_op jit(solution)/shard_map/while
  133.0 21.7 %copy-start.11 = (f32[1024]{0:T(1024)}, f32[1024]{0:T(1024)S(1)}, u32[]{:S(2)}) copy-start(f32[1024]{0:T(1024)S(1)} %bitcast_multiply_fusion.8) | copy-start | bytes 12292 | tf_op jit(solution)/shard_map/while
  177.7 25.3 %copy-start.15 = (f32[256]{0:T(256)}, f32[256]{0:T(256)S(1)}, u32[]{:S(2)}) copy-start(f32[256]{0:T(256)S(1)} %get-tuple-element.785) | copy-start | bytes 3076 | tf_op jit(solution)/shard_map/while
  177.7 25.3 %copy-start.16 = (f32[256]{0:T(256)}, f32[256]{0:T(256)S(1)}, u32[]{:S(2)}) copy-start(f32[256]{0:T(256)S(1)} %get-tuple-element.782) | copy-start | bytes 3076 | tf_op jit(solution)/shard_map/while
  180.7 21.3 %copy-start.5 = (f32[9,8,128]{2,0,1:T(8,128)}, f32[9,8,128]{2,0,1:T(8,128)S(1)}, u32[]{:S(2)}) copy-start(f32[9,8,128]{2,0,1:T(8,128)S(1)} %select_bitcast_fusion.2) | copy-start | bytes 110596 | tf_op jit(solution)/shard_map/while
  181.3 21.8 %copy-start.7 = (f32[1,8,128]{2,0,1:T(1,128)}, f32[1,8,128]{2,0,1:T(1,128)S(1)}, u32[]{:S(2)}) copy-start(f32[1,8,128]{2,0,1:T(1,128)S(1)} %get-tuple-element.786) | copy-start | bytes 12292 | tf_op jit(solution)/shard_map/while
  181.4 21.7 %copy-start.11 = (f32[1024]{0:T(1024)}, f32[1024]{0:T(1024)S(1)}, u32[]{:S(2)}) copy-start(f32[1024]{0:T(1024)S(1)} %bitcast_multiply_fusion.8) | copy-start | bytes 12292 | tf_op jit(solution)/shard_map/while
  226.2 25.3 %copy-start.15 = (f32[256]{0:T(256)}, f32[256]{0:T(256)S(1)}, u32[]{:S(2)}) copy-start(f32[256]{0:T(256)S(1)} %get-tuple-element.785) | copy-start | bytes 3076 | tf_op jit(solution)/shard_map/while
  226.2 25.3 %copy-start.16 = (f32[256]{0:T(256)}, f32[256]{0:T(256)S(1)}, u32[]{:S(2)}) copy-start(f32[256]{0:T(256)S(1)} %get-tuple-element.782) | copy-start | bytes 3076 | tf_op jit(solution)/shard_map/while
  229.7 21.8 %copy-start.7 = (f32[1,8,128]{2,0,1:T(1,128)}, f32[1,8,128]{2,0,1:T(1,128)S(1)}, u32[]{:S(2)}) copy-start(f32[1,8,128]{2,0,1:T(1,128)S(1)} %get-tuple-element.786) | copy-start | bytes 12292 | tf_op jit(solution)/shard_map/while
  229.8 21.7 %copy-start.11 = (f32[1024]{0:T(1024)}, f32[1024]{0:T(1024)S(1)}, u32[]{:S(2)}) copy-start(f32[1024]{0:T(1024)S(1)} %bitcast_multiply_fusion.8) | copy-start | bytes 12292 | tf_op jit(solution)/shard_map/while
  266.2 32.0 %copy-start.14 = (f32[9,8,128]{2,1,0:T(8,128)S(1)}, f32[9,8,128]{2,1,0:T(8,128)}, u32[]{:S(2)}) copy-start(f32[9,8,128]{2,1,0:T(8,128)} %get-tuple-element.441) | copy-start | bytes 110596
  268.2 26.0 %all-to-all-start.2 = ((f32[128,8,128]{2,1,0:T(8,128)}), f32[128,8,128]{2,1,0:T(8,128)S(1)}, u32[]{:S(2)}, u32[]{:S(2)}) async-start(f32[128,8,128]{2,1,0:T(8,128)} %bitcast.11), calls=%async_computation.2 | async-start | bytes 1048576 | tf_op jit(solution)/shard_map/all_to_all | solution.py:132
  276.3 281.4 %all-reduce.11.cloned.1.call-start = ((), (), s32[]{:S(2)}) async-start(), calls=%async_computation.4 | async-start | bytes 524288 | tf_op jit(solution)/shard_map/psum | solution.py:139
  277.0 282.3 %all-gather.3.cloned.1.call-start = ((), (), s32[]{:S(2)}) async-start(), calls=%async_computation.5 | async-start | bytes 2621440 | tf_op jit(solution)/shard_map/all_gather | solution.py:136
  299.3 26.9 %all-to-all-start.3 = ((f32[9,128,8]{0,2,1:T(8,128)}), f32[9,128,8]{0,2,1:T(8,128)S(1)}, u32[]{:S(2)}, u32[]{:S(2)}) async-start(f32[9,128,8]{0,2,1:T(8,128)} %bitcast.14), calls=%async_computation.3 | async-start | bytes 1048576 | tf_op jit(solution)/shard_map/all_to_all | solution.py:131
  (66 other events, 331.2 us)
Sparse Core Ops, SparseCore 0:
  282.7 274.9 all-reduce.10
Sparse Core Ops, SparseCore 1:
  298.3 29.1 all-gather.2
